TPU v7x, 256 devices: a whole 4x4x8 slice. The times are simulated.
256 devices in a mesh: tile: 32 (over z_hi, y, core), lev: 8 (over x, z_lo).
Axes of the slice: x: 4, y: 4, z: 8 (z_hi: 4, z_lo: 2; z = z_hi * 2 + z_lo), core: 2. Of those that a mesh axis runs over, the one named last changes fastest.
Arguments:
- tracer_start: float32 [48, 2048, 720], P('lev', 'tile'), may hold values from -6 to 6
- wind_row: float32 [48, 2048, 720], P('lev', 'tile'), may hold values from -0.16 to 0.16
- wind_col: float32 [48, 2048, 720], P('lev', 'tile'), may hold values from -0.16 to 0.16
- diffusivity: float32 [48, 2048, 720], P('lev', 'tile'), may hold values from 0.01 to 0.16
- flux: float32 [11520, 128], P(('tile', 'lev')), may hold values from -6 to 6
- remap_weights: float32 [23040, 128, 128], P(('tile', 'lev')), may hold values from -0.5 to 0.5
- remap_tile: int32 [23040, 1], P(('tile', 'lev')), may hold values from 0 to 31; in each aligned block of 90 rows (0 to 89, 90 to 179, ...) at most 8 rows name the same one
- remap_block: int32 [23040], P(('tile', 'lev')), may hold values from 0 to 359
- profiles: float32 [64, 48], P(None, 'lev'), may hold values from -0.875 to 0.875
- sound_count: int32 [32], P('tile'), may hold values from 1 to 2048, 32768 in all
- sound_col: int32 [65536], P('tile'), may hold values from 0 to 46079
- sound_prof: int32 [65536], P('tile'), may hold values from 0 to 63
- sound_obs: float32 [65536], P('tile'), may hold values from -8 to 8
- sound_sigma: float32 [65536], P('tile'), may hold values from 0.5 to 2
Outputs:
- modeled: float32 [65536], P('tile')
- misfit: float32 [65536], P('tile')
- state_gradient: float32 [48, 2048, 720], P('lev', 'tile')
- flux_gradient: float32 [11520, 128], P(('tile', 'lev'))
Inputs may be any that keep to these rules, and one draw needn't show every extreme that they name: `remap_tile`: within the (90) entries of one device no tile is named more than 8 times, a bound that some block reaches. `sound_count`: some tile has exactly 2048 live soundings.
All inputs are finite; a program needn't handle non-finite values. No bound on the sum of `sound_count` on one device may be relied on, other than what follows from the above.
Results may differ from a plain program's by a relative error of at most 0.0003.
Values sent between devices are 32-bit elements; how exact they have to be, the bound alone decides.
A program may use at most 128 MiB of HBM per device.

v0:
```python
import jax
import jax.numpy as jnp
from jax import lax
from jax.sharding import PartitionSpec as P

highest = lax.Precision.HIGHEST


def with_halo(cells, sides, width):
    for axis, dim in sides:
        count = lax.axis_size(axis)
        ends = count - 1
        head = lax.slice_in_dim(cells, 0, width, axis=dim)
        tail = lax.slice_in_dim(cells, cells.shape[dim] - width, cells.shape[dim], axis=dim)
        cells = jnp.concatenate(
            [
                lax.ppermute(tail, axis, [(i, (i + 1) % count) for i in range(ends)]),
                cells,
                lax.ppermute(head, axis, [((i + 1) % count, i) for i in range(ends)]),
            ],
            axis=dim,
        )
    return cells


def from_behind(value, axis, steps):
    count = lax.axis_size(axis)
    leading, last = (max(0, -steps), min(count, count - steps))
    return lax.ppermute(value, axis, [(source, source + steps) for source in range(leading, last)])


def spread(block, axis, holder):
    block = jnp.where(lax.axis_index(axis) == holder, block, jnp.zeros_like(block))
    return lax.psum(block, axis)


def apply_step(field, above, below, upper, lower, coeffs, adjoint):
    rise, rise_low, cross, cross_left, mixing, mixing_low = coeffs
    right = jnp.roll(field, -1, axis=2)
    left = jnp.roll(field, 1, axis=2)
    rise_pos = jnp.maximum(rise, 0.0)
    rise_neg = jnp.minimum(rise, 0.0)
    low_pos = jnp.maximum(rise_low, 0.0)
    low_neg = jnp.minimum(rise_low, 0.0)
    cross_pos = jnp.maximum(cross, 0.0)
    cross_neg = jnp.minimum(cross, 0.0)
    left_pos = jnp.maximum(cross_left, 0.0)
    left_neg = jnp.minimum(cross_left, 0.0)
    diffusion = mixing * (above - field) - mixing_low * (field - below)
    if adjoint:
        rows_term = rise_pos * (upper - field) - low_neg * (lower - field)
        cols_term = cross_pos * (right - field) - left_neg * (left - field)
    else:
        rows_term = low_pos * lower + low_neg * field - rise_pos * field - rise_neg * upper
        cols_term = left_pos * left + left_neg * field - cross_pos * field - cross_neg * right
    return field + rows_term + cols_term + diffusion


def transport(field, coeffs, adjoint):
    padded = with_halo(field, (("tile", 1), ("lev", 0)), 1)
    above = padded[2:, 1:-1, :]
    below = padded[:-2, 1:-1, :]
    upper = padded[1:-1, 2:, :]
    lower = padded[1:-1, :-2, :]
    return apply_step(field, above, below, upper, lower, coeffs, adjoint)


def on_device(
    tracer_start,
    wind_row,
    wind_col,
    diffusivity,
    flux,
    remap_weights,
    remap_tile,
    remap_block,
    profiles,
    sound_count,
    sound_col,
    sound_prof,
    sound_obs,
    sound_sigma,
):
    levels, rows, cols = tracer_start.shape
    entries, block_size, flux_cells = remap_weights.shape
    blocks = rows * cols // block_size
    tiles = lax.axis_size("tile")
    tile_index = lax.axis_index("tile")
    lev_index = lax.axis_index("lev")
    row_ids = lax.broadcasted_iota(jnp.int32, (1, rows, 1), 1)
    top_row = (row_ids == rows - 1) & (tile_index == tiles - 1)
    rise = jnp.where(top_row, 0.0, wind_row)
    rise_edge = from_behind(rise[:, rows - 1, :], "tile", 1)
    rise_low = jnp.concatenate([rise_edge[:, None, :], rise[:, : rows - 1, :]], axis=1)
    level_ids = lax.broadcasted_iota(jnp.int32, (levels, 1, 1), 0)
    top_level = (level_ids == levels - 1) & (lev_index == lax.axis_size("lev") - 1)
    mixing = jnp.where(top_level, 0.0, diffusivity)
    mixing_edge = from_behind(mixing[levels - 1], "lev", 1)
    mixing_low = jnp.concatenate([mixing_edge[None], mixing[: levels - 1]], axis=0)
    cross_left = jnp.roll(wind_col, 1, axis=2)
    coeffs = (rise, rise_low, wind_col, cross_left, mixing, mixing_low)
    flux_rep = jnp.repeat(flux, 2, axis=0)
    contrib = jnp.einsum(
        "ecf,ef->ec", remap_weights, flux_rep, precision=highest, preferred_element_type=jnp.float32
    )
    target = remap_tile[:, 0]
    global_rows = target * blocks + remap_block
    count = lax.axis_size("tile") * blocks
    local = global_rows
    inside = (local >= 0) & (local < count)
    summed = jax.ops.segment_sum(contrib, jnp.where(inside, local, count), num_segments=count + 1)
    partial_value = lax.psum_scatter(summed[:count], "tile", scatter_dimension=0, tiled=True)
    state = transport(tracer_start, coeffs, False)
    surface = lax.psum(partial_value, "lev").reshape(rows, cols)
    emission = jnp.where(lev_index == 0, surface, 0.0)
    state = state.at[0].add(emission)
    state = transport(state, coeffs, False)
    state = state.at[0].add(emission)
    slots = sound_col.shape[0]
    live = lax.iota(jnp.int32, slots) < sound_count[0]
    chooser = (sound_prof[:, None] == lax.iota(jnp.int32, profiles.shape[0])[None, :]).astype(
        jnp.float32
    )
    weights = jnp.dot(chooser, profiles, precision=highest, preferred_element_type=jnp.float32)
    flat = state.reshape(levels, rows * cols)
    values = jnp.take(flat, sound_col, axis=1)
    partial_column = jnp.sum(weights * values.T, axis=1)
    column = lax.psum(partial_column, "lev")
    modeled = jnp.where(live, column, 0.0)
    scaled = (column - sound_obs) / sound_sigma
    size_abs = jnp.abs(scaled)
    huber = jnp.where(size_abs <= 1.0, 0.5 * scaled * scaled, size_abs - 0.5)
    misfit = jnp.where(live, huber, 0.0)
    slope = jnp.where(live, jnp.clip(scaled, -1.0, 1.0) / sound_sigma, 0.0)
    adjoint_two = (
        jnp.zeros((levels, rows * cols), jnp.float32)
        .at[:, sound_col]
        .add((weights * slope[:, None]).T)
    )
    adjoint_two = adjoint_two.reshape(levels, rows, cols)
    adjoint_one = transport(adjoint_two, coeffs, True)
    surface_bar = (adjoint_two[0] + adjoint_one[0]).reshape(blocks, block_size)
    shared = spread(surface_bar, "lev", 0)
    piece = lax.all_gather(shared, "tile", axis=0, tiled=True)
    local = global_rows
    inside = (local >= 0) & (local < piece.shape[0])
    found = piece[jnp.clip(local, 0, piece.shape[0] - 1)]
    picked = jnp.where(inside[:, None], found, 0.0)
    state_gradient = transport(adjoint_one, coeffs, True)
    per_entry = jnp.einsum(
        "ecf,ec->ef", remap_weights, picked, precision=highest, preferred_element_type=jnp.float32
    )
    flux_gradient = per_entry.reshape(-1, 2, flux_cells).sum(axis=1)
    return (modeled, misfit, state_gradient, flux_gradient)


def solution(mesh):
    in_specs = (
        P("lev", "tile", None),
        P("lev", "tile", None),
        P("lev", "tile", None),
        P("lev", "tile", None),
        P(("tile", "lev"), None),
        P(("tile", "lev"), None, None),
        P(("tile", "lev"), None),
        P(("tile", "lev")),
        P(None, "lev"),
        P("tile"),
        P("tile"),
        P("tile"),
        P("tile"),
        P("tile"),
    )
    out_specs = (P("tile"), P("tile"), P("lev", "tile", None), P(("tile", "lev"), None))
    return jax.shard_map(
        on_device, mesh=mesh, in_specs=in_specs, out_specs=out_specs, check_vma=False
    )
```

profile of v0, /device:TPU:4, one launch (start us, length us, event | category | flops | bytes accessed | tf_op | source)
XLA Modules:
  0.0 526.2 jit_solution(2005856209609383764)
XLA Ops:
  8.4 11.2 %fusion.93 = f32[90,1,128]{2,1,0:T(1,128)S(1)} fusion(f32[90,128,128]{2,1,0:T(8,128)} %param.23, f32[90,128,1]{1,2,0:T(1,128)S(1)} %bitcast.55), kind=kOutput, calls=%fused_computation.180 | convolution fusion | flops 17694720 | bytes 5990400 | tf_op jit(solution)/shard_map/ecf,ef->ec/dot_general | solution.py:103
  19.6 3.8 scatter_custom_fusion
  23.3 4.5 slice.304
  33.5 3.9 collective-permute-start
  38.4 3.8 collective-permute-start.4
  55.9 78.7 %reduce-scatter.4.cloned.1.call-done = f32[360,128]{1,0:T(8,128)} async-done(((f32[11520,128]{1,0:T(8,128)}), f32[360,128]{1,0:T(8,128)}) %reduce-scatter.4.cloned.1.call-update) | async-done | bytes 184336
  135.5 6.5 %fusion.46 = f32[6,64,720]{2,1,0:T(8,128)S(1)} fusion(f32[6,64,720]{2,1,0:T(8,128)} %param.18, f32[1,66,720]{2,1,0:T(8,128)} %copy-done.30, f32[6,1,720]{2,1,0:T(1,128)} %collective-permute-done.2, f32[6,1,720]{2,1,0:T(1,128)} %collective-permute-done.1, f32[1,66,720]{2,1,0:T(8,128)} %copy-done.29, f32[6,64,719]{2,1,0:T(8,128)} %get-tuple-element.55, ...), kind=kLoop, calls=%fused_computation.76 | loop fusion | flops 12441600 | bytes 11473990 | tf_op jit(solution)/shard_map/add | solution.py:56
  142.1 68.7 %all-reduce.4.cloned.1.call-done = f32[360,128]{1,0:T(8,128)} async-done(((f32[360,128]{1,0:T(8,128)}), f32[360,128]{1,0:T(8,128)}) %all-reduce.4.cloned.1.call-update) | async-done | bytes 184336 | tf_op jit(solution)/shard_map/psum | solution.py:114
  229.5 6.2 %collective-permute-done.9 = f32[1,66,720]{2,1,0:T(8,128)S(1)} collective-permute-done((f32[1,66,720]{2,1,0:T(8,128)S(1)}, f32[1,66,720]{2,1,0:T(8,128)S(1)}, u32[]{:S(2)}, u32[]{:S(2)}) %collective-permute-start.9) | collective-permute-done | bytes 190112 | tf_op jit(solution)/shard_map/ppermute | solution.py:17
  235.8 3.6 fusion.33
  241.0 11.9 %copy.79 = f32[6,64,720]{0,2,1:T(8,128)} copy(f32[6,64,720]{2,1,0:T(8,128)} %fusion.70) | data formatting | bytes 2211840 | tf_op jit(solution)/shard_map/scatter-add | solution.py:118
  252.9 13.2 %gather_fusion = f32[2048,6]{1,0:T(8,128)S(1)} fusion(f32[6,46080]{0,1:T(8,128)} %bitcast.49, s32[2048]{0:T(1024)S(1)} %get-tuple-element.64), kind=kCustom, calls=%fused_computation | custom fusion | bytes 106496 | tf_op jit(solution)/shard_map/jit(_take)/gather | solution.py:126
  267.5 15.5 %psum.22 = f32[2048]{0:T(1024)S(1)} all-reduce(f32[2048]{0:T(1024)S(1)} %get-tuple-element.67), channel_id=1, replica_groups=mesh['tile'=32,'lev'=8] {'lev'}, use_global_device_ids=true, to_apply=%region_4.5 | all-reduce | flops 2048 | bytes 16384 | tf_op jit(solution)/shard_map/psum | solution.py:128
  284.0 20.8 %scatter_custom_fusion.1 = f32[6,46080]{0,1:T(8,128)} fusion(s32[2048]{0:T(1024)} %get-tuple-element.63, f32[2048,6]{1,0:T(8,128)S(1)} %copy.81, f32[]{:T(128)} %constant.93.clone.1), kind=kCustom, calls=%fused_computation.5 | custom fusion | flops 12288 | bytes 1106432 | tf_op jit(solution)/shard_map/scatter-add | solution.py:138
  304.9 11.9 %slice_reduce_fusion = f32[46080]{0:T(1024)} fusion(f32[6,46080]{0,1:T(8,128)} %scatter_custom_fusion.1), kind=kLoop, calls=%fused_computation.4 | loop fusion | bytes 368640 | tf_op jit(solution)/shard_map/slice | solution.py:142
  316.8 12.5 %copy.88 = f32[6,64,720]{2,1,0:T(8,128)S(1)} copy(f32[6,64,720]{0,2,1:T(8,128)} %bitcast.40) | data formatting | bytes 2211840 | tf_op jit(solution)/shard_map/reshape | solution.py:140
  332.5 4.5 collective-permute-done.10
  337.0 4.8 collective-permute-start.12
  346.1 6.0 %collective-permute-done.13 = f32[1,66,720]{2,1,0:T(8,128)S(1)} collective-permute-done((f32[1,66,720]{2,1,0:T(8,128)S(1)}, f32[1,66,720]{2,1,0:T(8,128)S(1)}, u32[]{:S(2)}, u32[]{:S(2)}) %collective-permute-start.13) | collective-permute-done | bytes 190112 | tf_op jit(solution)/shard_map/ppermute | solution.py:17
  356.5 80.2 %all-reduce.6.cloned.1.call-done = f32[360,128]{1,0:T(8,128)} async-done(((f32[360,128]{1,0:T(8,128)}), f32[360,128]{1,0:T(8,128)}) %all-reduce.6.cloned.1.call-update) | async-done | bytes 184336 | tf_op jit(solution)/shard_map/psum | solution.py:34
  445.5 3.6 collective-permute-start.17
  452.1 8.2 %collective-permute-done.17 = f32[1,66,720]{2,1,0:T(8,128)S(1)} collective-permute-done((f32[1,66,720]{2,1,0:T(8,128)S(1)}, f32[1,66,720]{2,1,0:T(8,128)S(1)}, u32[]{:S(2)}, u32[]{:S(2)}) %collective-permute-start.17) | collective-permute-done | bytes 190112 | tf_op jit(solution)/shard_map/ppermute | solution.py:17
  463.6 45.0 %all-gather.2.cloned.1.call-done = f32[11520,128]{1,0:T(8,128)} async-done(((f32[360,128]{1,0:T(8,128)}), f32[11520,128]{1,0:T(8,128)}) %all-gather.2.cloned.1.call-update) | async-done | bytes 5898256 | tf_op jit(solution)/shard_map/all_gather | solution.py:144
  512.0 7.0 %fusion.76 = f32[90,1,128]{2,1,0:T(1,128)S(1)} fusion(f32[90,128,128]{2,1,0:T(8,128)} %param.23, f32[90,128,1]{1,0,2:T(8,128)S(1)} %select_bitcast_fusion), kind=kOutput, calls=%fused_computation.147 | convolution fusion | flops 17694720 | bytes 5990400 | tf_op jit(solution)/shard_map/ecf,ec->ef/dot_general | solution.py:150
  (167 shorter events, 74.7 us)
Async XLA Ops:
  7.2 127.4 %reduce-scatter.4.cloned.1.call-start = ((), (), s32[]{:S(2)}) async-start(), calls=%async_computation.4 | async-start | bytes 6082560
  27.9 182.9 %all-reduce.4.cloned.1.call-start = ((), (), s32[]{:S(2)}) async-start(), calls=%async_computation.1 | async-start | bytes 368640 | tf_op jit(solution)/shard_map/psum | solution.py:114
  29.6 15.8 %collective-permute-start.1 = (f32[6,1,720]{2,1,0:T(1,128)}, f32[6,1,720]{2,1,0:T(1,128)}, u32[]{:S(2)}, u32[]{:S(2)}) collective-permute-start(f32[6,1,720]{2,1,0:T(1,128)} %get-tuple-element.58), channel_id=1, source_target_pairs={{0,8},{8,16},{16,24},{24,32},{32,40},{40,48},{48,56},{56,64},{64,7... | collective-permute-start | bytes 51848 | tf_op jit(solution)/shard_map/ppermute | solution.py:17
  32.0 13.5 %collective-permute-start.2 = (f32[6,1,720]{2,1,0:T(1,128)}, f32[6,1,720]{2,1,0:T(1,128)}, u32[]{:S(2)}, u32[]{:S(2)}) collective-permute-start(f32[6,1,720]{2,1,0:T(1,128)} %get-tuple-element.59), channel_id=1, source_target_pairs={{8,0},{16,8},{24,16},{32,24},{40,32},{48,40},{56,48},{64,56},{72,6... | collective-permute-start | bytes 51848 | tf_op jit(solution)/shard_map/ppermute | solution.py:19
  33.5 202.2 %copy-start.3 = (f32[6,64,720]{2,1,0:T(8,128)}, f32[6,64,720]{2,1,0:T(8,128)S(1)}, u32[]{:S(2)}) copy-start(f32[6,64,720]{2,1,0:T(8,128)S(1)} %broadcast_select_fusion.1) | copy-start | bytes 3317764
  33.5 21.8 %collective-permute-start = (f32[6,720]{1,0:T(8,128)S(1)}, f32[6,720]{1,0:T(8,128)S(1)}, u32[]{:S(2)}, u32[]{:S(2)}) collective-permute-start(f32[6,720]{1,0:T(8,128)S(1)} %bitcast.56), channel_id=1, source_target_pairs={{0,8},{8,16},{16,24},{24,32},{32,40},{40,48},{48,56},{56,64},{64,7... | collective-permute-start | bytes 51848 | tf_op jit(solution)/shard_map/ppermute | solution.py:29
  38.4 96.3 %collective-permute-start.4 = (f32[64,720]{1,0:T(8,128)}, f32[64,720]{1,0:T(8,128)S(1)}, u32[]{:S(2)}, u32[]{:S(2)}) collective-permute-start(f32[64,720]{1,0:T(8,128)} %slice_bitcast_fusion), channel_id=1, source_target_pairs={{0,1},{1,2},{2,3},{3,4},{4,5},{5,6},{6,7},{8,9},{9,10},{10,11},{11... | collective-permute-start | bytes 552968 | tf_op jit(solution)/shard_map/ppermute | solution.py:29
  46.2 88.5 %collective-permute-start.3 = (f32[1,66,720]{2,1,0:T(8,128)S(1)}, f32[1,66,720]{2,1,0:T(8,128)S(1)}, u32[]{:S(2)}, u32[]{:S(2)}) collective-permute-start(f32[1,66,720]{2,1,0:T(8,128)S(1)} %get-tuple-element.34), channel_id=1, source_target_pairs={{1,0},{2,1},{3,2},{4,3},{5,4},{6,5},{7,6},{9,8},{10,9},{11,10},{12... | collective-permute-start | bytes 570248 | tf_op jit(solution)/shard_map/ppermute | solution.py:19
  49.3 85.5 %collective-permute-start.5 = (f32[1,66,720]{2,1,0:T(8,128)S(1)}, f32[1,66,720]{2,1,0:T(8,128)S(1)}, u32[]{:S(2)}, u32[]{:S(2)}) collective-permute-start(f32[1,66,720]{2,1,0:T(8,128)S(1)} %get-tuple-element.35), channel_id=1, source_target_pairs={{0,1},{1,2},{2,3},{3,4},{4,5},{5,6},{6,7},{8,9},{9,10},{10,11},{11... | collective-permute-start | bytes 570248 | tf_op jit(solution)/shard_map/ppermute | solution.py:17
  134.6 302.1 %all-reduce.6.cloned.1.call-start = ((), (), s32[]{:S(2)}) async-start(), calls=%async_computation.2 | async-start | bytes 368640 | tf_op jit(solution)/shard_map/psum | solution.py:34
  214.3 3.1 collective-permute-start.6
  215.6 4.8 collective-permute-start.7
  220.4 9.1 %collective-permute-start.8 = (f32[1,66,720]{2,1,0:T(8,128)S(1)}, f32[1,66,720]{2,1,0:T(8,128)S(1)}, u32[]{:S(2)}, u32[]{:S(2)}) collective-permute-start(f32[1,66,720]{2,1,0:T(8,128)S(1)} %get-tuple-element.32), channel_id=1, source_target_pairs={{1,0},{2,1},{3,2},{4,3},{5,4},{6,5},{7,6},{9,8},{10,9},{11,10},{12... | collective-permute-start | bytes 570248 | tf_op jit(solution)/shard_map/ppermute | solution.py:19
  222.9 12.8 %collective-permute-start.9 = (f32[1,66,720]{2,1,0:T(8,128)S(1)}, f32[1,66,720]{2,1,0:T(8,128)S(1)}, u32[]{:S(2)}, u32[]{:S(2)}) collective-permute-start(f32[1,66,720]{2,1,0:T(8,128)S(1)} %get-tuple-element.33), channel_id=1, source_target_pairs={{0,1},{1,2},{2,3},{3,4},{4,5},{5,6},{6,7},{8,9},{9,10},{10,11},{11... | collective-permute-start | bytes 570248 | tf_op jit(solution)/shard_map/ppermute | solution.py:17
  329.4 3.1 collective-permute-start.11
  330.7 6.2 %collective-permute-start.10 = (f32[6,1,720]{2,1,0:T(1,128)S(1)}, f32[6,1,720]{2,1,0:T(1,128)S(1)}, u32[]{:S(2)}, u32[]{:S(2)}) collective-permute-start(f32[6,1,720]{2,1,0:T(1,128)S(1)} %get-tuple-element.47), channel_id=1, source_target_pairs={{8,0},{16,8},{24,16},{32,24},{40,32},{48,40},{56,48},{64,56},{72,6... | collective-permute-start | bytes 51848 | tf_op jit(solution)/shard_map/ppermute | solution.py:19
  337.0 9.1 %collective-permute-start.12 = (f32[1,66,720]{2,1,0:T(8,128)S(1)}, f32[1,66,720]{2,1,0:T(8,128)S(1)}, u32[]{:S(2)}, u32[]{:S(2)}) collective-permute-start(f32[1,66,720]{2,1,0:T(8,128)S(1)} %get-tuple-element.30), channel_id=1, source_target_pairs={{1,0},{2,1},{3,2},{4,3},{5,4},{6,5},{7,6},{9,8},{10,9},{11,10},{12... | collective-permute-start | bytes 570248 | tf_op jit(solution)/shard_map/ppermute | solution.py:19
  341.8 10.2 %collective-permute-start.13 = (f32[1,66,720]{2,1,0:T(8,128)S(1)}, f32[1,66,720]{2,1,0:T(8,128)S(1)}, u32[]{:S(2)}, u32[]{:S(2)}) collective-permute-start(f32[1,66,720]{2,1,0:T(8,128)S(1)} %get-tuple-element.31), channel_id=1, source_target_pairs={{0,1},{1,2},{2,3},{3,4},{4,5},{5,6},{6,7},{8,9},{9,10},{10,11},{11... | collective-permute-start | bytes 570248 | tf_op jit(solution)/shard_map/ppermute | solution.py:17
  354.6 82.2 %copy-start.36 = (s32[90]{0:T(128)S(1)}, s32[90]{0:T(128)}, u32[]{:S(2)}) copy-start(s32[90]{0:T(128)} %param.25) | copy-start | bytes 1084
  356.5 152.2 %all-gather.2.cloned.1.call-start = ((), (), s32[]{:S(2)}) async-start(), calls=%async_computation.3 | async-start | bytes 6082560 | tf_op jit(solution)/shard_map/all_gather | solution.py:144
  436.9 3.1 collective-permute-start.15
  438.2 4.8 collective-permute-start.14
  443.0 9.1 %collective-permute-start.16 = (f32[1,66,720]{2,1,0:T(8,128)S(1)}, f32[1,66,720]{2,1,0:T(8,128)S(1)}, u32[]{:S(2)}, u32[]{:S(2)}) collective-permute-start(f32[1,66,720]{2,1,0:T(8,128)S(1)} %get-tuple-element.28), channel_id=1, source_target_pairs={{1,0},{2,1},{3,2},{4,3},{5,4},{6,5},{7,6},{9,8},{10,9},{11,10},{12... | collective-permute-start | bytes 570248 | tf_op jit(solution)/shard_map/ppermute | solution.py:19
  445.5 14.8 %collective-permute-start.17 = (f32[1,66,720]{2,1,0:T(8,128)S(1)}, f32[1,66,720]{2,1,0:T(8,128)S(1)}, u32[]{:S(2)}, u32[]{:S(2)}) collective-permute-start(f32[1,66,720]{2,1,0:T(8,128)S(1)} %get-tuple-element.29), channel_id=1, source_target_pairs={{0,1},{1,2},{2,3},{3,4},{4,5},{5,6},{6,7},{8,9},{9,10},{10,11},{11... | collective-permute-start | bytes 570248 | tf_op jit(solution)/shard_map/ppermute | solution.py:17
  (38 other events, 700.1 us)
Sparse Core Ops, SparseCore 0:
  28.0 106.5 reduce-scatter.3
  137.2 73.5 all-reduce.3
  356.6 80.1 all-reduce.5
  439.2 69.3 all-gather.1
where the time goes:
time: 529 us; the launch traced here: 526 us
  waiting for transfers between devices  312 us (59%)
  local copies, waits for them, and re-layouts  70.2 us (13%)
  other arithmetic  50.4 us (10%)
  starting transfers between devices  43.9 us (8%)
  matrix products  19.1 us (4%)
  blocking collectives  15.5 us (3%)
  between operations  15.3 us (3%)
    psum x1, waiting for transfers between devices, spread(): return lax.psum(block, axis)  80.2 us
    unnamed x5, waiting for transfers between devices  78.7 us
    psum x1, waiting for transfers between devices, on_device(): surface = lax.psum(partial_value, 'lev').reshape(rows, cols)  68.7 us
    all_gather x1, waiting for transfers between devices, on_device(): piece = lax.all_gather(shared, 'tile', axis=0, tiled=True)  45 us
    scatter-add x1, other arithmetic, on_device(): adjoint_two = jnp.zeros((levels, rows * cols), jnp.float32).at[:, sound_c...  20.8 us
    ppermute x8, waiting for transfers between devices, with_halo(): lax.ppermute(tail, axis, [(i, (i + 1) % count) for i in range(ends)])  20.4 us
    ppermute x8, waiting for transfers between devices, with_halo(): lax.ppermute(head, axis, [((i + 1) % count, i) for i in range(ends)])  18.7 us
    ppermute x8, starting transfers between devices, with_halo(): lax.ppermute(tail, axis, [(i, (i + 1) % count) for i in range(ends)])  18 us
  transfers between devices with their start and end apart: 22, of which 13 were waited for; matrix products, arithmetic and copies ran while one was open for 4% of the time, Pallas kernels for 0%

commit v1 on v0

v1 whole, which is shorter than its diff:
```python
import functools

import jax
import jax.numpy as jnp
from jax import lax
from jax.experimental import pallas as pl
from jax.experimental.pallas import tpu as pltpu
from jax.sharding import PartitionSpec as P

MESH = pl.DeviceIdType.MESH
f32 = jnp.float32
bf16 = jnp.bfloat16
NT_DIMS = (((1,), (1,)), ((), ()))
SLOT = 8
CH = 256


def split2(x):
    hi = x.astype(bf16)
    return hi, (x - hi.astype(f32)).astype(bf16)


def dot(a, b):
    return jnp.dot(a, b, preferred_element_type=f32)


def dot_nt(a, b):
    return lax.dot_general(a, b, NT_DIMS, preferred_element_type=f32)


def iota(shape, dim):
    return lax.broadcasted_iota(jnp.int32, shape, dim)


def rcopy(src, dst, ss, rs, dev):
    return pltpu.make_async_remote_copy(
        src_ref=src, dst_ref=dst, send_sem=ss, recv_sem=rs, device_id=dev, device_id_type=MESH
    )


def sizes_of(shapes):
    levels, rows, cols = shapes[0]
    return levels, rows, cols


def body(
    dims,
    tr_h, wr_h, wc_h, df_h, w_h,
    flux, tcol, trow, brow, prof, cnt, scol, sprof, sobs, ssig,
    modeled, misfit, grad, fgrad,
    t_v, wr, wc, mx, w_v, wcat, contrib, sbuf, rbuf, sid, rid, pbuf,
    pk0u, pk0d, rb0lo, rb0hi, pk1u, pk1d, rb1lo, rb1hi, pk2u, pk2d, rb2lo, rb2hi,
    pk3u, pk3d, rb3lo, rb3hi,
    ct, amat, gmat, s1, s2, rowi, w8, qv, cbuf, slope_v, a2, bs, a1, surf6, blk, bout, bin_, picked,
    sem_in, s_lv, r_lv, s_pr, r_pr, s_r0, r_r0, s_a, r_a, s_i, r_i, s_q, r_q,
    s_r1, r_r1, s_c, r_c, s_r2, r_r2, s_l1, r_l1, s_r3, r_r3, s_b, r_b,
):
    NT, NL, L, R, C, S, NE, CPG = dims
    NP = NE // 2
    NB = R * C // 128
    SL = NT * SLOT
    NG = max(1, NT // 16)
    LG = min(128, SL)
    NCH = NP // CPG
    t = lax.axis_index("tile")
    l = lax.axis_index("lev")
    tup, tdn = lax.rem(t + 1, NT), lax.rem(t + NT - 1, NT)
    lup, ldn = lax.rem(l + 1, NL), lax.rem(l + NL - 1, NL)

    barrier = pltpu.get_barrier_semaphore()

    def sig_t(d, _):
        pl.semaphore_signal(barrier, inc=1, device_id={"tile": lax.rem(t + d, NT)}, device_id_type=MESH)
        return 0

    def sig_l(d, _):
        pl.semaphore_signal(barrier, inc=1, device_id={"lev": lax.rem(l + d, NL)}, device_id_type=MESH)
        return 0

    lax.fori_loop(1, NT, sig_t, 0)
    lax.fori_loop(1, NL, sig_l, 0)

    loads = [
        pltpu.make_async_copy(tr_h, t_v.at[pl.ds(1, L)], sem_in.at[0]),
        pltpu.make_async_copy(wr_h, wr, sem_in.at[1]),
        pltpu.make_async_copy(wc_h, wc, sem_in.at[2]),
        pltpu.make_async_copy(df_h, mx.at[pl.ds(1, L)], sem_in.at[3]),
    ]

    def wload(i):
        part = pl.ds(2 * CPG * i, 2 * CPG)
        return pltpu.make_async_copy(w_h.at[part], w_v.at[part], sem_in.at[4 + i])

    loads[0].start()
    loads[1].start()
    for i in range(NCH):
        wload(i).start()
    loads[2].start()
    loads[3].start()

    pl.semaphore_wait(barrier, NT - 1 + NL - 1)

    planes = [
        rcopy(tr_h.at[L - 1], t_v.at[0], s_lv.at[0], r_lv.at[0], {"lev": lup}),
        rcopy(tr_h.at[0], t_v.at[L + 1], s_lv.at[1], r_lv.at[1], {"lev": ldn}),
        rcopy(df_h.at[L - 1], mx.at[0], s_lv.at[2], r_lv.at[2], {"lev": lup}),
    ]
    for c in planes:
        c.start()

    def prof_copy(to, slot):
        return rcopy(prof, pbuf.at[slot], s_pr.at[to], r_pr.at[slot], {"lev": to})

    def prof_send(d, _):
        to = lax.rem(l + d, NL)
        prof_copy(to, l).start()
        return 0

    lax.fori_loop(1, NL, prof_send, 0)
    pbuf[l] = prof[...]

    def pair_copies(pku, pkd, lo, hi, ss, rs):
        return [
            rcopy(pku, lo, ss.at[0], rs.at[0], {"tile": tup}),
            rcopy(pkd, hi, ss.at[1], rs.at[1], {"tile": tdn}),
        ]

    loads[0].wait()
    loads[1].wait()
    top = jnp.where(t == NT - 1, 0.0, 1.0).astype(f32)
    low_ok = jnp.where(t == 0, 0.0, 1.0).astype(f32)
    pk0u[...] = jnp.zeros_like(pk0u)
    pk0d[...] = jnp.zeros_like(pk0d)
    for k in range(L):
        wr[k, R - 1 : R, :] = wr[k, R - 1 : R, :] * top
        pk0u[k : k + 1, :] = t_v[k + 1, R - 1 : R, :]
        pk0u[8 + k : 9 + k, :] = wr[k, R - 1 : R, :]
        pk0d[k : k + 1, :] = t_v[k + 1, 0:1, :]
    rows0 = pair_copies(pk0u, pk0d, rb0lo, rb0hi, s_r0, r_r0)
    for c in rows0:
        c.start()

    r16 = iota((16, 2 * 128), 0)
    l16 = iota((16, 2 * 128), 1)

    def contrib_step(i, _):
        wload(i).wait()
        outs = []
        for p in range(CPG):
            f = i * CPG + p
            w2 = w_v[pl.ds(2 * f, 2)].reshape(256, 128)
            hi, lo = split2(w2)
            wc2 = jnp.concatenate([hi, lo], axis=1)
            wcat[f] = wc2
            row = flux[pl.ds(f, 1), :]
            fh = row.astype(bf16).astype(f32)
            fl = row - fh
            both = jnp.where(
                r16 == 0,
                jnp.concatenate([fh, fh], axis=1),
                jnp.where((r16 == 1) & (l16 < 128), jnp.concatenate([fl, fl], axis=1), 0.0),
            )
            got = dot_nt(both.astype(bf16), wc2)
            outs.append(got[0:1] + got[1:2])
        for p in range(CPG):
            f = i * CPG + p
            contrib[pl.ds(2 * f, 1), :] = outs[p][:, :128]
            contrib[pl.ds(2 * f + 1, 1), :] = outs[p][:, 128:]
        return 0

    lax.fori_loop(0, NCH, contrib_step, 0)

    tr_row, tr_col = trow[...], tcol[...]
    same = tr_col == tr_row
    sub, lan = iota((NE, NE), 0), iota((NE, NE), 1)
    rank_row = jnp.sum(jnp.where(same & (sub < lan), 1.0, 0.0), axis=0, keepdims=True)
    rank_col = jnp.sum(jnp.where(same & (lan < sub), 1.0, 0.0), axis=1, keepdims=True)
    sel_row = tr_row * SLOT + rank_row.astype(jnp.int32)
    sel_col = tr_col * SLOT + rank_col.astype(jnp.int32)
    place = jnp.where(iota((SL, NE), 0) == sel_row, 1.0, 0.0).astype(bf16)
    ch, cl = split2(contrib[...])
    slots = dot(place, ch) + dot(place, cl)
    sbuf[...] = slots.reshape(NT, SLOT, 128)
    base = lax.rem(t, 16) * SLOT
    spot = jnp.where(iota((NE, 128), 1) == rank_col.astype(jnp.int32) + base, 1.0, 0.0).astype(bf16)
    at_tile = iota((NT, NE), 0) == tr_row
    bid = brow[...] + 1
    bid_hi = jnp.where(bid >= 256, 256.0, 0.0)
    bid_lo = bid.astype(f32) - bid_hi
    ids = dot(jnp.where(at_tile, bid_hi, 0.0).astype(bf16), spot) + dot(
        jnp.where(at_tile, bid_lo, 0.0).astype(bf16), spot
    )
    sid[...] = ids.reshape(NT, 1, 128)

    def a_copy(to, slot):
        return rcopy(sbuf.at[to], rbuf.at[slot], s_a.at[to], r_a.at[slot], {"tile": to})

    def i_copy(to, slot):
        return rcopy(sid.at[to], rid.at[slot], s_i.at[to], r_i.at[slot], {"tile": to})

    def a2a_send(d, _):
        to = lax.rem(t + d, NT)
        i_copy(to, t).start()
        a_copy(to, t).start()
        return 0

    lax.fori_loop(1, NT, a2a_send, 0)
    rbuf[t] = sbuf[t]
    rid[t] = sid[t]

    cell = scol[...]
    row_s = ((cell.astype(f32) + 0.5) * (1.0 / C)).astype(jnp.int32)
    col_s = cell - row_s * C
    rowi[...] = row_s

    def ct_step(i, _):
        off = pl.multiple_of(i * 16, 16)
        ct[pl.ds(off, 16), :] = jnp.where(iota((16, S), 0) + off == col_s, 1.0, 0.0).astype(bf16)
        return 0

    lax.fori_loop(0, ct.shape[0] // 16, ct_step, 0)

    def prof_wait(d, _):
        src = lax.rem(l + d, NL)
        prof_copy(src, src).wait_recv()
        return 0

    lax.fori_loop(1, NL, prof_wait, 0)
    pm = jnp.concatenate([pbuf[ldn][L - 1 : L], pbuf[l][0:L], pbuf[lup][0:1]], axis=0)
    p_hi = pm.astype(bf16)
    rest = pm - p_hi.astype(f32)
    p_mid = rest.astype(bf16)
    p_lo = rest - p_mid.astype(f32)
    pm3 = jnp.concatenate([p_hi.astype(f32), p_mid.astype(f32), p_lo, jnp.zeros_like(p_lo)], axis=0).astype(bf16)
    pick = jnp.where(iota((128, S), 0) == sprof[...], 1.0, 0.0).astype(bf16)
    w24 = dot(pm3, pick)
    w8[...] = w24[0:8] + w24[8:16] + w24[16:24]

    loads[2].wait()
    loads[3].wait()
    for c in rows0:
        c.wait_recv()
    rb0lo[8:16, :] = rb0lo[8:16, :] * low_ok
    mx[L] = mx[L] * jnp.where(l == NL - 1, 0.0, 1.0).astype(f32)
    QR = 80 + 3 * R

    def put_g(at, value, total):
        n = value.shape[0]
        hi, lo = split2(value)
        gmat[at : at + n, :] = hi
        gmat[total + at : total + at + n, :] = lo

    RS = R + 16
    rise_x = jnp.concatenate([rb0lo[8:9, :], wr[0], jnp.zeros((15, C), f32)], axis=0)
    wc0 = wc[0]
    QT = RS + 3 * R
    put_g(0, rise_x, QT)
    put_g(RS, wc0, QT)
    put_g(RS + R, jnp.roll(wc0, 1, axis=1), QT)
    put_g(RS + 2 * R, mx[1], QT)
    idx = iota((RS, CH), 0)
    idr = iota((R, CH), 0)

    def q_step(j, _):
        lanes = pl.ds(pl.multiple_of(j * CH, CH), CH)
        v2 = dot(gmat[0 : 2 * QT, :], ct[0:C, lanes])
        v = v2[:QT] + v2[QT:]
        r = rowi[:, lanes]
        vx = v[:RS]
        rise_s = jnp.sum(jnp.where(idx == r + 1, vx, 0.0), axis=0, keepdims=True)
        low_s = jnp.sum(jnp.where(idx == r, vx, 0.0), axis=0, keepdims=True)
        mine = idr == r

        def at(o):
            return jnp.sum(jnp.where(mine, v[o : o + R], 0.0), axis=0, keepdims=True)

        cross_s, left_s, mix_s = at(RS), at(RS + R), at(RS + 2 * R)
        p0, p1 = w8[1:2, lanes], w8[2:3, lanes]
        low_neg, low_pos = jnp.minimum(low_s, 0.0), jnp.maximum(low_s, 0.0)
        left_neg, left_pos = jnp.minimum(left_s, 0.0), jnp.maximum(left_s, 0.0)
        self_c = 2.0 + low_neg - jnp.maximum(rise_s, 0.0) + left_neg - jnp.maximum(cross_s, 0.0) - mix_s
        qv[0:1, lanes] = p0 * self_c + p1 * mix_s
        qv[1:2, lanes] = p0 * low_pos
        qv[2:3, lanes] = -p0 * jnp.minimum(rise_s, 0.0)
        qv[3:4, lanes] = p0 * left_pos
        qv[4:5, lanes] = -p0 * jnp.minimum(cross_s, 0.0)
        return 0

    def q_copy(to):
        return rcopy(qv, qv, s_q.at[to], r_q.at[0], {"lev": to})

    @pl.when(l == 0)
    def _():
        qv[...] = jnp.zeros_like(qv)
        lax.fori_loop(0, S // CH, q_step, 0)

        def q_send(d, _):
            q_copy(lax.rem(l + d, NL)).start()
            return 0

        lax.fori_loop(1, NL, q_send, 0)

    for c in planes:
        c.wait_recv()
    mx[0] = mx[0] * jnp.where(l == 0, 0.0, 1.0).astype(f32)

    def shifted(get, i, lo_row, hi_row):
        c = get(8 * i, 8)
        lower = jnp.concatenate([lo_row, c[:7]], axis=0) if i == 0 else get(8 * i - 1, 8)
        upper = jnp.concatenate([c[1:], hi_row], axis=0) if i == R // 8 - 1 else get(8 * i + 1, 8)
        return c, lower, upper

    def stencil(k, get, get_above, get_below, lo_row, hi_row, adjoint, put):
        rl = rb0lo[pl.ds(8 + k, 1), :]
        for i in range(R // 8):
            c, lower, upper = shifted(get, i, lo_row, hi_row)
            rows = pl.ds(8 * i, 8)
            rise = wr[k, rows, :]
            if i == 0:
                rise_low = jnp.concatenate([rl, rise[:7]], axis=0)
            else:
                rise_low = wr[k, pl.ds(8 * i - 1, 8), :]
            cross = wc[k, rows, :]
            cross_left = jnp.roll(cross, 1, axis=1)
            right = jnp.roll(c, -1, axis=1)
            left = jnp.roll(c, 1, axis=1)
            m = mx[k + 1, rows, :]
            ml = mx[k, rows, :]
            above = get_above(8 * i)
            below = get_below(8 * i)
            if adjoint:
                v = jnp.maximum(rise, 0.0) * (upper - c) - jnp.minimum(rise_low, 0.0) * (lower - c)
                v += jnp.maximum(cross, 0.0) * (right - c) - jnp.minimum(cross_left, 0.0) * (left - c)
            else:
                v = jnp.maximum(rise_low, 0.0) * lower + jnp.minimum(rise_low, 0.0) * c
                v -= jnp.maximum(rise, 0.0) * c + jnp.minimum(rise, 0.0) * upper
                v += jnp.maximum(cross_left, 0.0) * left + jnp.minimum(cross_left, 0.0) * c
                v -= jnp.maximum(cross, 0.0) * c + jnp.minimum(cross, 0.0) * right
            v = c + v + m * (above - c) - ml * (c - below)
            put(rows, v)

    def at_level(ref, k):
        return lambda o, n=8: ref[k, pl.ds(o, n), 0:C]

    def fwd1(k, _):
        def put(rows, v):
            s1[k + 1, rows, :] = v

        stencil(
            k, at_level(t_v, k + 1), at_level(t_v, k + 2), at_level(t_v, k),
            rb0lo[pl.ds(k, 1), :], rb0hi[pl.ds(k, 1), :], False, put,
        )
        return 0

    lax.fori_loop(0, L, fwd1, 0)
    s1[0] = jnp.zeros((R, C), f32)
    s1[L + 1] = jnp.zeros((R, C), f32)

    def a2a_wait(d, _):
        src = lax.rem(t + d, NT)
        i_copy(src, src).wait_recv()
        a_copy(src, src).wait_recv()
        return 0

    lax.fori_loop(1, NT, a2a_wait, 0)
    got_id = rid[...].reshape(NT, 128)
    per = NT // NG
    id_rows = [
        jnp.sum(got_id[g * per : (g + 1) * per], axis=0, keepdims=True)[:, :LG] - 1.0 for g in range(NG)
    ]
    id_row = jnp.concatenate(id_rows, axis=1)
    owner = jnp.where(iota((NB, SL), 0).astype(f32) == id_row, 1.0, 0.0).astype(bf16)
    rh, rl_ = split2(rbuf[...].reshape(SL, 128))
    blk[...] = dot(owner, rh) + dot(owner, rl_)
    NGR = R // 8
    per_g = NB // NGR
    for r in range(8):
        q, o = divmod(C * r, 128)
        width = min(per_g - q, C // 128 + 2)
        parts = [blk[pl.ds(q + i, NGR, stride=per_g), :] for i in range(width)]
        while len(parts) < C // 128 + 2:
            parts.append(jnp.zeros((NGR, 128), f32))
        v = jnp.concatenate(parts, axis=1)
        if o:
            v = pltpu.roll(v, v.shape[1] - o, 1)
        for j in range(surf6.shape[0]):
            surf6.at[j][pl.ds(r, NGR, stride=8), :] = v[:, 128 * j : 128 * j + 128]
    surf = jnp.concatenate([surf6[j] for j in range(surf6.shape[0])], axis=1)[:, :C]
    pk1u[...] = jnp.zeros_like(pk1u)
    pk1d[...] = jnp.zeros_like(pk1d)
    for k in range(L):
        pk1u[k : k + 1, :] = s1[k + 1, R - 1 : R, :]
        pk1d[k : k + 1, :] = s1[k + 1, 0:1, :]
    pk1u[L : L + 1, :] = surf[R - 1 : R]
    pk1d[L : L + 1, :] = surf[0:1]
    rows1 = pair_copies(pk1u, pk1d, rb1lo, rb1hi, s_r1, r_r1)
    for c in rows1:
        c.start()

    GT = (L + 2) * R + RS + 2 * R
    o_s = (L + 2) * R
    put_g(0, mx[0] * s1[1], GT)
    put_g((L + 1) * R, mx[L] * s1[L], GT)
    put_g(o_s + RS, jnp.roll(surf, 1, axis=1), GT)
    put_g(o_s + RS + R, jnp.roll(surf, -1, axis=1), GT)
    for c in rows1:
        c.wait_recv()
    put_g(o_s, jnp.concatenate([rb1lo[L : L + 1, :], surf, rb1hi[L : L + 1, :], jnp.zeros((14, C), f32)], axis=0), GT)

    def fwd2(k, _):
        def put(rows, v):
            s2[rows, :] = v

        stencil(
            k, at_level(s1, k + 1), at_level(s1, k + 2), at_level(s1, k),
            rb1lo[pl.ds(k, 1), :], rb1hi[pl.ds(k, 1), :], False, put,
        )
        hi, lo = split2(s2[...])
        gmat[pl.ds(pl.multiple_of((k + 1) * R, 16), R), :] = hi
        gmat[pl.ds(pl.multiple_of(GT + (k + 1) * R, 16), R), :] = lo
        return 0

    lax.fori_loop(0, L, fwd2, 0)

    @pl.when(l != 0)
    def _():
        q_copy(0).wait_recv()

    def coef_of(r, lanes, scale):
        c = jnp.where(idx == r + 1, scale * qv[0:1, lanes], 0.0)
        c += jnp.where(idx == r, scale * qv[1:2, lanes], 0.0)
        return c + jnp.where(idx == r + 2, scale * qv[2:3, lanes], 0.0)

    def gather_step(j, _):
        lanes = pl.ds(pl.multiple_of(j * CH, CH), CH)
        v2 = dot(gmat[0 : 2 * GT, :], ct[0:C, lanes])
        v = v2[:GT] + v2[GT:]
        r = rowi[:, lanes]
        acc = qv[3:4, lanes] * v[o_s + RS : o_s + RS + R] + qv[4:5, lanes] * v[o_s + RS + R : GT]
        for k in range(L + 2):
            acc += w8[k : k + 1, lanes] * v[k * R : (k + 1) * R]
        part = jnp.sum(jnp.where(idr == r, acc, 0.0), axis=0, keepdims=True)
        part += jnp.sum(v[o_s : o_s + RS] * coef_of(r, lanes, 1.0), axis=0, keepdims=True)
        slope_v[:, lanes] = part
        return 0

    lax.fori_loop(0, S // CH, gather_step, 0)
    cbuf[l] = slope_v[...]

    def c_copy(to, slot):
        return rcopy(slope_v, cbuf.at[slot], s_c.at[to], r_c.at[slot], {"lev": to})

    def c_send(d, _):
        c_copy(lax.rem(l + d, NL), l).start()
        return 0

    def c_wait(d, _):
        src = lax.rem(l + d, NL)
        c_copy(src, src).wait_recv()
        return 0

    def c_sent(d, _):
        c_copy(lax.rem(l + d, NL), l).wait_send()
        return 0

    lax.fori_loop(1, NL, c_send, 0)
    lax.fori_loop(1, NL, c_wait, 0)
    column = cbuf[0]
    for i in range(1, NL):
        column = column + cbuf[i]
    live = iota((1, S), 1) < cnt[...]
    modeled[...] = jnp.where(live, column, 0.0)
    sigma = ssig[...]
    scaled = (column - sobs[...]) / sigma
    size_abs = jnp.abs(scaled)
    misfit[...] = jnp.where(live, jnp.where(size_abs <= 1.0, 0.5 * scaled * scaled, size_abs - 0.5), 0.0)
    slope = jnp.where(live, jnp.clip(scaled, -1.0, 1.0) / sigma, 0.0)
    lax.fori_loop(1, NL, c_sent, 0)
    slope_v[...] = slope

    def put_a(at, lanes, value):
        n = value.shape[0]
        hi, lo = split2(value)
        amat[at : at + n, lanes] = hi
        amat[GT + at : GT + at + n, lanes] = lo

    def a_step(j, _):
        lanes = pl.ds(pl.multiple_of(j * CH, CH), CH)
        r = rowi[:, lanes]
        sl = slope_v[:, lanes]
        mine = idr == r
        for k in range(L + 2):
            put_a(k * R, lanes, jnp.where(mine, sl * w8[k : k + 1, lanes], 0.0))
        put_a(o_s, lanes, coef_of(r, lanes, sl))
        put_a(o_s + RS, lanes, jnp.where(mine, sl * qv[3:4, lanes], 0.0))
        put_a(o_s + RS + R, lanes, jnp.where(mine, sl * qv[4:5, lanes], 0.0))
        return 0

    lax.fori_loop(0, S // CH, a_step, 0)

    def scatter_step(j, _):
        off = pl.multiple_of(j * CH, CH)
        v2 = dot_nt(amat[...], ct[pl.ds(off, CH), :])
        v = v2[:GT] + v2[GT:]
        a2[:, :, pl.ds(off, CH)] = v[:o_s].reshape(L + 2, R, CH)
        bs[:, pl.ds(off, CH)] = v[o_s:]
        return 0

    lax.fori_loop(0, ct.shape[0] // CH, scatter_step, 0)
    pk2u[...] = jnp.zeros_like(pk2u)
    pk2d[...] = jnp.zeros_like(pk2d)
    for k in range(L):
        pk2u[k : k + 1, :] = a2[k + 1, R - 1 : R, 0:C]
        pk2d[k : k + 1, :] = a2[k + 1, 0:1, 0:C]
    pk2u[L : L + 1, :] = bs[R + 1 : R + 2, 0:C]
    pk2d[L : L + 1, :] = bs[0:1, 0:C]
    rows2 = pair_copies(pk2u, pk2d, rb2lo, rb2hi, s_r2, r_r2)
    for c in rows2:
        c.start()
    bar = bs[1 : R + 1, 0:C]
    bar += jnp.roll(bs[RS : RS + R, 0:C], -1, axis=1) + jnp.roll(bs[RS + R : RS + 2 * R, 0:C], 1, axis=1)
    for c in rows2:
        c.wait_recv()

    def adj1(k):
        def put(rows, v):
            a1[k + 1, rows, :] = v

        stencil(
            k, at_level(a2, k + 1), at_level(a2, k + 2), at_level(a2, k),
            rb2lo[pl.ds(k, 1), :], rb2hi[pl.ds(k, 1), :], True, put,
        )

    def adj1_step(k, _):
        adj1(k)
        return 0

    def adj1_ends(i, _):
        adj1(i * (L - 1))
        return 0

    lax.fori_loop(0, 2, adj1_ends, 0)
    planes1 = [
        rcopy(a1.at[L], a1.at[0], s_l1.at[0], r_l1.at[0], {"lev": lup}),
        rcopy(a1.at[1], a1.at[L + 1], s_l1.at[1], r_l1.at[1], {"lev": ldn}),
    ]

    rid_ = iota((R, C), 0)
    bar += jnp.where(rid_ == 0, rb2lo[L : L + 1, :], 0.0) + jnp.where(rid_ == R - 1, rb2hi[L : L + 1, :], 0.0)
    wide = jnp.concatenate([bar, jnp.zeros((R, 128 * surf6.shape[0] - C), f32)], axis=1)
    for j in range(surf6.shape[0]):
        surf6[j] = wide[:, 128 * j : 128 * j + 128]
    lines = []
    for r in range(8):
        lines.append(
            jnp.concatenate(
                [surf6.at[j][pl.ds(r, NGR, stride=8), :] for j in range(surf6.shape[0])], axis=1
            )
        )
    for q in range(per_g):
        r, c = divmod(128 * q, C)
        if c + 128 <= C:
            piece = lines[r][:, c : c + 128]
        else:
            piece = jnp.concatenate([lines[r][:, c:C], lines[r + 1][:, : c + 128 - C]], axis=1)
        blk[pl.ds(q, NGR, stride=per_g), :] = piece
    bh, bl = split2(blk[...])
    for g in range(NG):
        spread = jnp.broadcast_to(id_rows[g], (128, LG)).T
        want = jnp.concatenate([spread] * (-(-NB // 128)), axis=1)[:, :NB]
        mine = jnp.where(iota((LG, NB), 1).astype(f32) == want, 1.0, 0.0).astype(bf16)
        back = dot(mine, bh) + dot(mine, bl)
        bout[g * per : (g + 1) * per] = back.reshape(per, SLOT, 128)

    def b_copy(to, slot):
        return rcopy(bout.at[to], bin_.at[slot], s_b.at[to], r_b.at[slot], {"tile": to})

    def b_send(d, _):
        b_copy(lax.rem(t + d, NT), t).start()
        return 0

    lax.fori_loop(1, NT, b_send, 0)
    bin_[t] = bout[t]
    for c in planes1:
        c.start()
    lax.fori_loop(1, L - 1, adj1_step, 0)
    pk3u[...] = jnp.zeros_like(pk3u)
    pk3d[...] = jnp.zeros_like(pk3d)
    for k in range(L):
        pk3u[k : k + 1, :] = a1[k + 1, R - 1 : R, :]
        pk3d[k : k + 1, :] = a1[k + 1, 0:1, :]
    rows3 = pair_copies(pk3u, pk3d, rb3lo, rb3hi, s_r3, r_r3)
    for c in rows3:
        c.start()

    def b_wait(d, _):
        src = lax.rem(t + d, NT)
        b_copy(src, src).wait_recv()
        return 0

    lax.fori_loop(1, NT, b_wait, 0)
    take = jnp.where(iota((NE, SL), 1) == sel_col, 1.0, 0.0).astype(bf16)
    gh, gl = split2(bin_[...].reshape(SL, 128))
    picked[...] = dot(take, gh) + dot(take, gl)

    def fgrad_step(i, _):
        outs = []
        for p in range(CPG):
            f = i * CPG + p
            row = jnp.concatenate([picked[pl.ds(2 * f, 1), :], picked[pl.ds(2 * f + 1, 1), :]], axis=1)
            fh = row.astype(bf16).astype(f32)
            both = jnp.where(r16 == 0, fh, jnp.where(r16 == 1, row - fh, 0.0)).astype(bf16)
            got = dot(both, wcat[f])
            outs.append(got[0:1, :128] + got[0:1, 128:] + got[1:2, :128])
        for p in range(CPG):
            fgrad[pl.ds(i * CPG + p, 1), :] = outs[p]
        return 0

    lax.fori_loop(0, NCH, fgrad_step, 0)

    for c in rows3:
        c.wait_recv()
    for c in planes1:
        c.wait_recv()

    def grad_step(k, _):
        def put(rows, v):
            grad[k, rows, :] = v

        stencil(
            k, at_level(a1, k + 1), at_level(a1, k + 2), at_level(a1, k),
            rb3lo[pl.ds(k, 1), :], rb3hi[pl.ds(k, 1), :], True, put,
        )
        return 0

    lax.fori_loop(0, L, grad_step, 0)

    for c in planes + rows0 + rows1 + rows2 + planes1 + rows3:
        c.wait_send()

    def lev_sent(d, _):
        prof_copy(lax.rem(l + d, NL), l).wait_send()
        return 0

    lax.fori_loop(1, NL, lev_sent, 0)

    @pl.when(l == 0)
    def _():
        def q_sent(d, _):
            q_copy(lax.rem(l + d, NL)).wait_send()
            return 0

        lax.fori_loop(1, NL, q_sent, 0)

    def tile_sent(d, _):
        to = lax.rem(t + d, NT)
        i_copy(to, t).wait_send()
        a_copy(to, t).wait_send()
        b_copy(to, t).wait_send()
        return 0

    lax.fori_loop(1, NT, tile_sent, 0)


def on_device(NT, NL, tr, wr, wc, df, flux, w, rtile, rblock, profiles, cnt, scol, sprof, sobs, ssig):
    L, R, C = tr.shape
    NE = w.shape[0]
    S = scol.shape[0]
    NP = NE // 2
    CPG = 5 if NP % 5 == 0 else 1
    SL = NT * SLOT
    NB = R * C // 128
    CP = -(-C // 256) * 256
    CK = -(-C // 128)
    RS = R + 16
    GT = (L + 2) * R + RS + 2 * R
    any_, vm = pl.BlockSpec(memory_space=pl.ANY), pl.BlockSpec(memory_space=pltpu.VMEM)
    V = pltpu.VMEM
    D = pltpu.SemaphoreType.DMA
    scratch = [
        V((L + 2, R, C), f32), V((L, R, C), f32), V((L, R, C), f32), V((L + 1, R, C), f32),
        V(w.shape, f32), V((NP, 256, 256), bf16), V((NE, 128), f32),
        V((NT, SLOT, 128), f32), V((NT, SLOT, 128), f32), V((NT, 1, 128), f32), V((NT, 1, 128), f32),
        V((NL, 8, 128), f32),
        V((16, C), f32), V((8, C), f32), V((16, C), f32), V((8, C), f32),
        V((8, C), f32), V((8, C), f32), V((8, C), f32), V((8, C), f32),
        V((8, C), f32), V((8, C), f32), V((8, C), f32), V((8, C), f32),
        V((8, C), f32), V((8, C), f32), V((8, C), f32), V((8, C), f32),
        V((CP, S), bf16), V((2 * GT, S), bf16), V((2 * GT, C), bf16),
        V((L + 2, R, C), f32), V((R, C), f32), V((1, S), jnp.int32), V((8, S), f32), V((8, S), f32),
        V((NL, 1, S), f32), V((1, S), f32), V((L + 2, R, CP), f32), V((RS + 2 * R, CP), f32),
        V((L + 2, R, C), f32), V((CK, R, 128), f32), V((NB, 128), f32),
        V((NT, SLOT, 128), f32), V((NT, SLOT, 128), f32), V((NE, 128), f32),
        D((4 + NP // CPG,)), D((3,)), D((3,)), D((NL,)), D((NL,)), D((2,)), D((2,)),
        D((NT,)), D((NT,)), D((NT,)), D((NT,)), D((NL,)), D((1,)),
        D((2,)), D((2,)), D((NL,)), D((NL,)), D((2,)), D((2,)), D((2,)), D((2,)), D((2,)), D((2,)),
        D((NT,)), D((NT,)),
    ]
    prof = jnp.pad(profiles.T, ((0, 8 - L), (0, 128 - profiles.shape[0])))
    modeled, misfit, grad, fgrad = pl.pallas_call(
        functools.partial(body, (NT, NL, L, R, C, S, NE, CPG)),
        out_shape=[
            jax.ShapeDtypeStruct((1, S), f32),
            jax.ShapeDtypeStruct((1, S), f32),
            jax.ShapeDtypeStruct((L, R, C), f32),
            jax.ShapeDtypeStruct((NP, 128), f32),
        ],
        in_specs=[any_] * 5 + [vm] * 10,
        out_specs=[vm] * 4,
        scratch_shapes=scratch,
        compiler_params=pltpu.CompilerParams(
            collective_id=0, has_side_effects=True, vmem_limit_bytes=63000 * 1024
        ),
    )(
        tr, wr, wc, df, w, flux, rtile, rtile.reshape(1, NE), rblock.reshape(1, NE), prof,
        cnt.reshape(1, 1), scol.reshape(1, S), sprof.reshape(1, S), sobs.reshape(1, S), ssig.reshape(1, S),
    )
    return modeled.reshape(S), misfit.reshape(S), grad, fgrad


def solution(mesh):
    both = ("tile", "lev")
    field = P("lev", "tile", None)
    in_specs = (
        field, field, field, field, P(both, None), P(both, None, None), P(both, None), P(both),
        P(None, "lev"), P("tile"), P("tile"), P("tile"), P("tile"), P("tile"),
    )
    out_specs = (P("tile"), P("tile"), field, P(both, None))
    return jax.shard_map(
        functools.partial(on_device, mesh.shape["tile"], mesh.shape["lev"]),
        mesh=mesh, in_specs=in_specs, out_specs=out_specs, check_vma=False,
    )
```

time: 529 us -> 90.6 us (0.17)
  waiting for transfers between devices: 312 us -> 0 us
  Pallas kernels: 0 us -> 80.7 us
  local copies, waits for them, and re-layouts: 70.2 us -> 8.25 us
  other arithmetic: 50.4 us -> 0 us
  starting transfers between devices: 43.9 us -> 0 us
  matrix products: 19.1 us -> 0 us
  blocking collectives: 15.5 us -> 0 us
  between operations: 15.3 us -> 1.29 us
    psum x2 -> x0, waiting for transfers between devices: 149 us -> none  [the longest x1 80.2 us: spread(): return lax.psum(block, axis)]
    pallas_call x0 -> x1, Pallas kernels: none -> 80.7 us  [on_device(): pl.pallas_call(functools.partial(body, (NT, NL, L, R, C, S, NE, CPG)), ou...]
    unnamed x5 -> x0, waiting for transfers between devices: 78.7 us -> none
    all_gather x1 -> x0, waiting for transfers between devices: 45 us -> none  [on_device(): piece = lax.all_gather(shared, 'tile', axis=0, tiled=True)]
    ppermute x18 -> x0, starting transfers between devices: 43.7 us -> none  [the longest x8 18 us: with_halo(): lax.ppermute(tail, axis, [(i, (i + 1) % count) for i in range(ends)])]
    ppermute x18 -> x0, waiting for transfers between devices: 39.1 us -> none  [the longest x8 20.4 us: with_halo(): lax.ppermute(tail, axis, [(i, (i + 1) % count) for i in range(ends)])]
    scatter-add x4 -> x0, other arithmetic: 27.2 us -> none  [the longest x1 20.8 us: on_device(): adjoint_two = jnp.zeros((levels, rows * cols), jnp.float32).at[:, sound_c...]
    slice x18 -> x0, local copies, waits for them, and re-layouts: 24.3 us -> none  [the longest x2 11.9 us: on_device(): surface_bar = (adjoint_two[0] + adjoint_one[0]).reshape(blocks, block_size)]
  transfers between devices with their start and end apart: 22 -> 0, of which waited for: 13 -> 0; matrix products, arithmetic and copies ran while one was open for 4% -> 0% of each run, Pallas kernels for 0% -> 0%
where the time goes in v1:
time: 90.6 us; the launch traced here: 90.3 us
  Pallas kernels  80.7 us (89%)
  local copies, waits for them, and re-layouts  8.25 us (9%)
  between operations  1.29 us (1%)
    pallas_call x1, Pallas kernels, on_device(): pl.pallas_call(functools.partial(body, (NT, NL, L, R, C, S, NE, CPG)), ou...  80.7 us
    unnamed x7, local copies, waits for them, and re-layouts  6.97 us

profile of v1, /device:TPU:4, one launch (start us, length us, event | category | flops | bytes accessed | tf_op | source)
XLA Modules:
  0.0 90.3 jit_solution(3641486098171024178)
XLA Ops:
  1.3 1.3 %pad.4.prof = f32[8,128]{1,0:T(8,128)} pad(f32[6,64]{1,0:T(8,128)} %bitcast.17, f32[]{:T(128)} %constant.2.clone.1), padding=0_2x0_64 | pad | bytes 5636 | tf_op jit(solution)/shard_map/jit(_pad)/pad | solution.py:699
  2.6 1.4 %copy.18.tcol = s32[90,1]{1,0:T(8,128)} copy(s32[90,1]{0,1:T(1,128)} %param.20) | data formatting | bytes 720 | tf_op args[6]
  3.9 80.7 %shard_map.165 = (f32[1,2048]{1,0:T(1,128)}, f32[1,2048]{1,0:T(1,128)}, f32[6,64,720]{2,1,0:T(8,128)}, f32[45,128]{1,0:T(8,128)}) custom-call(f32[6,64,720]{2,1,0:T(8,128)} %tr_h.1, f32[6,64,720]{2,1,0:T(8,128)} %wr_h.1, f32[6,64,720]{2,1,0:T(8,128)} %wc_h.1, f32[6,64,720]{2,1,0:T(8,128)} %df_h.1, f32[90,128,128]{2,1,0:T(8,128)} %w_h.1, f32[45,128]{1,0:T(8,128)} %flux.1, ...), custom_call_target="tpu_custom_call" | custom-call | tf_op jit(solution)/shard_map/pallas_call | solution.py:700
  84.7 1.3 %copy.24 = f32[2048]{0:T(1024)} copy(f32[2048]{0:T(1024)} %bitcast.16) | data formatting | bytes 16384
  86.0 1.3 %copy.25 = f32[2048]{0:T(1024)} copy(f32[2048]{0:T(1024)} %bitcast.15) | data formatting | bytes 16384
  87.3 0.0 copy-start
  87.3 2.4 %copy.26 = f32[6,64,720]{2,1,0:T(8,128)} copy(f32[6,64,720]{2,1,0:T(8,128)} %get-tuple-element.18) | data formatting | bytes 2211840
  89.7 0.0 copy-done
  89.7 0.6 copy.27
Async XLA Ops:
  87.3 2.4 %copy-start = (f32[45,128]{1,0:T(8,128)S(1)}, f32[45,128]{1,0:T(8,128)}, u32[]{:S(2)}) copy-start(f32[45,128]{1,0:T(8,128)} %get-tuple-element.19) | copy-start | bytes 69124
